TPU v7x, 32 devices: a whole 2x2x4 slice. The times are simulated.
32 devices in a mesh: dp: 4 (over y, x), fsdp: 8 (over z, core).
Axes of the slice: x: 2, y: 2, z: 4, core: 2. Of those that a mesh axis runs over, the one named last changes fastest.
Arguments:
- hidden: bfloat16 [16384, 1536], P(('dp', 'fsdp')), may hold values from -6 to 6
- lengths: int32 [512], P(('dp', 'fsdp')), may hold values from 1 to 32
- norm_gain: float32 [1536], replicated, may hold values from 0.1 to 1.9
- up_weight: bfloat16 [1536, 3072], P('fsdp'), may hold values from -0.15625 to 0.15625
- down_weight: bfloat16 [3072, 1536], P('fsdp'), may hold values from -0.109375 to 0.109375
- pool_gain: float32 [1536], replicated, may hold values from 0.1 to 1.9
- proj_weight: bfloat16 [1536, 768], P('fsdp'), may hold values from -1 to 1
- owners: int32 [512, 1], P(('dp', 'fsdp')), may hold values from 0 to 3; in each aligned block of 16 rows (0 to 15, 16 to 31, ...) at most 8 rows name the same one
Outputs:
- owned: bfloat16 [1024, 768], P(('dp', 'fsdp'))
Inputs may be any that keep to these rules, and one draw needn't show every extreme that they name: `owners`: in each aligned block of 16 passages no owner is named by more than 8 passages, a bound that some block reaches.
All inputs are finite; a program needn't handle non-finite values.
Results may differ from a plain program's by a relative error of at most 0.014.
Values may be sent and summed in bfloat16 or wider, within the bound.
A program may use at most 128 MiB of HBM per device.

v0:
```python
import jax
import jax.numpy as jnp
from jax import lax
from jax.sharding import PartitionSpec as P

ITERS = 4
RIDGE_TERM = 1.0
EPSILON = 1e-06
PRECISE = lax.Precision.HIGHEST


def rms_scale(values, gain_vector):
    return (
        values
        * lax.rsqrt(jnp.mean(values * values, axis=-1, keepdims=True) + EPSILON)
        * gain_vector
    )


def build_covariance(full_sums, average_sum, row_count):
    average = average_sum / row_count
    eye_matrix = jnp.eye(full_sums.shape[0], dtype=jnp.float32)
    covariance = (
        full_sums / row_count - average[:, None] * average[None, :] + RIDGE_TERM * eye_matrix
    )
    magnitude = jnp.sqrt(jnp.sum(covariance * covariance))
    initial = 4.0 / magnitude * eye_matrix - 4.0 * covariance / (magnitude * magnitude)
    return (covariance, average, initial)


def newton_update(iterate_rows, covariance, iterate_full):
    mixed = jnp.dot(
        jnp.dot(iterate_rows, covariance, precision=PRECISE, preferred_element_type=jnp.float32),
        iterate_full,
        precision=PRECISE,
        preferred_element_type=jnp.float32,
    )
    return 2.0 * iterate_rows - mixed


def last_update_rows(centered, covariance, iterate_full):
    row_product = jnp.dot(
        centered, iterate_full, precision=PRECISE, preferred_element_type=jnp.float32
    )
    row_mixed = jnp.dot(
        jnp.dot(row_product, covariance, precision=PRECISE, preferred_element_type=jnp.float32),
        iterate_full,
        precision=PRECISE,
        preferred_element_type=jnp.float32,
    )
    return 2.0 * row_product - row_mixed


def on_device(hidden, lengths, norm_gain, up_weight, down_weight, pool_gain, proj_weight, owners):
    tok_rows = hidden.shape[0]
    pass_rows = lengths.shape[0]
    seq_len = tok_rows // pass_rows
    normed = rms_scale(hidden.astype(jnp.float32), norm_gain).astype(jnp.bfloat16)
    columns = normed
    hidden_pre = jnp.dot(
        columns,
        lax.all_gather(up_weight, "fsdp", axis=0, tiled=True),
        preferred_element_type=jnp.float32,
    )
    activated = jax.nn.gelu(hidden_pre, approximate=True).astype(jnp.bfloat16)
    columns = activated
    branch = jnp.dot(
        columns,
        lax.all_gather(down_weight, "fsdp", axis=0, tiled=True),
        preferred_element_type=jnp.float32,
    )
    layer_out = (hidden.astype(jnp.float32) + branch).astype(jnp.bfloat16)
    token_index = lax.broadcasted_iota(jnp.int32, (pass_rows, tok_rows), 1)
    passage_index = lax.broadcasted_iota(jnp.int32, (pass_rows, tok_rows), 0)
    inside = (token_index // seq_len == passage_index) & (token_index % seq_len < lengths[:, None])
    pooled = (
        jnp.dot(inside.astype(jnp.bfloat16), layer_out, preferred_element_type=jnp.float32)
        / lengths.astype(jnp.float32)[:, None]
    )
    pool_normed = rms_scale(pooled, pool_gain).astype(jnp.bfloat16)
    columns = pool_normed
    embedded = jnp.dot(
        columns,
        lax.all_gather(proj_weight, "fsdp", axis=0, tiled=True),
        preferred_element_type=jnp.float32,
    )
    products = jnp.dot(embedded.T, embedded, precision=PRECISE, preferred_element_type=jnp.float32)
    column_sum = jnp.sum(embedded, axis=0)
    total_rows = float(pass_rows * lax.axis_size("dp") * lax.axis_size("fsdp"))
    full_sums, average_sum = lax.psum((products, column_sum), ("dp", "fsdp"))
    covariance, average, iterate_full = build_covariance(full_sums, average_sum, total_rows)
    for iteration in range(ITERS - 2):
        iterate_full = newton_update(iterate_full, covariance, iterate_full)
    whitened = last_update_rows(embedded - average, covariance, iterate_full).astype(jnp.bfloat16)
    owner_count = lax.axis_size("dp")
    capacity = 2 * pass_rows // owner_count
    target_owner = owners[:, 0]
    position = lax.broadcasted_iota(jnp.int32, (pass_rows, pass_rows), 0)
    previous = lax.broadcasted_iota(jnp.int32, (pass_rows, pass_rows), 1)
    earlier = (target_owner[:, None] == target_owner[None, :]) & (previous < position)
    target = target_owner * capacity + jnp.sum(earlier.astype(jnp.int32), axis=1)
    slot_index = lax.broadcasted_iota(jnp.int32, (owner_count * capacity, pass_rows), 0)
    selector = (slot_index == target[None, :]).astype(jnp.bfloat16)
    outgoing = jnp.dot(selector, whitened, preferred_element_type=jnp.float32).astype(jnp.bfloat16)
    return lax.all_to_all(outgoing, "dp", split_axis=0, concat_axis=0, tiled=True)


def solution(mesh):
    placed = (
        P(("dp", "fsdp"), None),
        P(("dp", "fsdp")),
        P(),
        P("fsdp", None),
        P("fsdp", None),
        P(),
        P("fsdp", None),
        P(("dp", "fsdp"), None),
    )
    return jax.shard_map(
        on_device, mesh=mesh, in_specs=placed, out_specs=P(("dp", "fsdp"), None), check_vma=False
    )
```

profile of v0, /device:TPU:0, one launch (start us, length us, event | category | flops | bytes accessed | tf_op | source)
XLA Modules:
  0.0 415.3 jit_solution(10799612231338822403)
XLA Ops:
  6.5 0.0 copy-start.3
  6.5 0.0 copy-start.1
  6.5 0.0 copy-start.4
  6.5 0.0 all-gather.4.cloned.1.call-start
  6.5 0.7 all-gather.4.cloned.1.call-update
  7.3 0.0 all-gather.6.cloned.1.call-start
  7.3 0.7 all-gather.6.cloned.1.call-update
  8.0 0.0 all-gather.8.cloned.1.call-start
  8.1 0.7 all-gather.8.cloned.1.call-update
  8.7 0.0 all-reduce.2.cloned.1.call-start
  8.8 0.0 copy-done.3
  8.8 0.0 copy-done.1
  8.9 0.4 fusion.8
  9.3 0.0 copy-start.2
  9.3 93.2 %all-gather.4.cloned.1.call-done = bf16[1536,3072]{1,0:T(8,128)(2,1)} async-done(((bf16[192,3072]{1,0:T(8,128)(2,1)}), bf16[1536,3072]{1,0:T(8,128)(2,1)}) %all-gather.4.cloned.1.call-update) | async-done | bytes 9437200 | tf_op jit(solution)/shard_map/all_gather | solution.py:62
  102.5 90.9 %all-gather.6.cloned.1.call-done = bf16[3072,1536]{1,0:T(8,128)(2,1)} async-done(((bf16[384,1536]{1,0:T(8,128)(2,1)}), bf16[3072,1536]{1,0:T(8,128)(2,1)}) %all-gather.6.cloned.1.call-update) | async-done | bytes 9437200 | tf_op jit(solution)/shard_map/all_gather | solution.py:69
  193.3 0.0 copy-done.4
  193.3 16.5 %fusion.16 = bf16[512,1536]{1,0:T(8,128)(2,1)S(1)} fusion(bf16[3072,1536]{1,0:T(8,128)(2,1)} %all-gather.6.cloned.1.call-done, bf16[512,1536]{1,0:T(8,128)(2,1)S(1)} %copy-done.1, bf16[1536,3072]{1,0:T(8,128)(2,1)} %all-gather.4.cloned.1.call-done, f32[1536]{0:T(1024)S(1)} %copy-done.4, f32[512]{0:T(512)S(1)} %add_rsqrt_fusion), kind=kOutput, calls=%fused_computation.19 | convolution fusion | flops 9683337216 | bytes 22028288 | tf_op jit(solution)/shard_map/dot_general | solution.py:67
  209.8 0.5 multiply_reduce_fusion.1
  210.3 14.8 %all-gather.8.cloned.1.call-done = bf16[1536,768]{1,0:T(8,128)(2,1)} async-done(((bf16[192,768]{1,0:T(8,128)(2,1)}), bf16[1536,768]{1,0:T(8,128)(2,1)}) %all-gather.8.cloned.1.call-update) | async-done | bytes 2359312 | tf_op jit(solution)/shard_map/all_gather | solution.py:84
  225.1 0.0 copy-done.2
  225.1 2.1 fusion.73
  227.2 0.0 copy-start.5
  227.2 3.5 fusion.74
  230.7 0.0 all-reduce.2.cloned.1.call-update
  230.7 0.0 copy-done.5
  230.7 0.2 convert_reduce_fusion
  230.9 40.2 %psum.14 = f32[768]{0:T(1024)S(1)} all-reduce(f32[768]{0:T(1024)S(1)} %get-tuple-element.7), channel_id=1, replica_groups=mesh['dp'=4,'fsdp'=8] {'dp','fsdp'}, use_global_device_ids=true, to_apply=%region_4.5 | all-reduce | flops 768 | bytes 6144 | tf_op jit(solution)/shard_map/psum | solution.py:90
  271.2 94.1 %all-reduce.2.cloned.1.call-done = f32[768,768]{1,0:T(8,128)} async-done(((f32[768,768]{1,0:T(8,128)}), f32[768,768]{1,0:T(8,128)}) %all-reduce.2.cloned.1.call-update) | async-done | bytes 2359312 | tf_op jit(solution)/shard_map/psum | solution.py:90
  365.3 0.0 copy-start
  365.3 3.2 multiply_reduce_fusion
  369.2 0.0 copy-done
  369.3 6.7 %fusion.19 = f32[768,768]{1,0:T(8,128)S(1)} fusion(f32[]{:T(128)S(6)} %mul.135, f32[]{:T(128)S(6)} %div.58, f32[768,768]{1,0:T(8,128)S(1)} %copy-done, f32[768]{0:T(1024)S(1)} %broadcast_multiply_fusion), kind=kOutput, calls=%fused_computation.27 | convolution fusion | flops 5445255168 | bytes 4721672 | tf_op jit(solution)/shard_map/dot_general | solution.py:33
  376.0 6.9 %multiply_subtract_fusion.1 = f32[768,768]{1,0:T(8,128)S(1)} fusion(f32[768,768]{1,0:T(8,128)S(1)} %fusion.19, f32[]{:T(128)S(6)} %mul.135, f32[]{:T(128)S(6)} %div.58, f32[768]{0:T(1024)S(1)} %broadcast_multiply_fusion, f32[768,768]{1,0:T(8,128)S(1)} %copy-done), kind=kOutput, calls=%fused_computation.21 | convolution fusion | flops 5448794112 | bytes 7080968 | tf_op jit(solution)/shard_map/dot_general | solution.py:32
  382.9 6.4 %fusion.72 = f32[768,768]{1,0:T(8,128)S(1)} fusion(f32[768,768]{1,0:T(8,128)S(1)} %multiply_subtract_fusion.1, f32[768,768]{1,0:T(8,128)S(1)} %copy-done, f32[768]{0:T(1024)S(1)} %broadcast_multiply_fusion), kind=kOutput, calls=%fused_computation.89 | convolution fusion | flops 5439356928 | bytes 7080960 | tf_op jit(solution)/shard_map/dot_general | solution.py:33
  389.3 6.1 %multiply_subtract_fusion = f32[768,768]{1,0:T(8,128)S(1)} fusion(f32[768,768]{1,0:T(8,128)S(1)} %multiply_subtract_fusion.1, f32[768,768]{1,0:T(8,128)S(1)} %fusion.72), kind=kOutput, calls=%fused_computation.20 | convolution fusion | flops 5436997632 | bytes 7077888 | tf_op jit(solution)/shard_map/dot_general | solution.py:32
  395.4 1.5 fusion.41
  396.8 1.6 fusion.71
  398.4 1.3 fusion.39
  399.7 0.1 fusion.38
  399.8 8.1 %all_to_all.12 = bf16[4,8,768]{2,1,0:T(8,128)(2,1)S(1)} all-to-all(bf16[4,8,768]{2,1,0:T(8,128)(2,1)S(1)} %fusion.38), channel_id=1, replica_groups=mesh['dp'=4,'fsdp'=8] {'dp'}, dimensions={0} | all-to-all | bytes 98304 | tf_op jit(solution)/shard_map/all_to_all | solution.py:105
  407.9 0.6 copy.11
  (8 shorter events, 0.0 us)
Async XLA Ops:
  6.5 2.3 copy-start.3
  6.5 2.3 copy-start.1
  6.5 186.8 %copy-start.4 = (f32[1536]{0:T(1024)S(1)}, f32[1536]{0:T(1024)}, u32[]{:S(2)}) copy-start(f32[1536]{0:T(1024)} %param.10) | copy-start | bytes 18436
  6.5 95.9 %all-gather.4.cloned.1.call-start = ((), (), s32[]{:S(2)}) async-start(), calls=%async_computation.1 | async-start | bytes 10616832 | tf_op jit(solution)/shard_map/all_gather | solution.py:62
  7.3 186.1 %all-gather.6.cloned.1.call-start = ((), (), s32[]{:S(2)}) async-start(), calls=%async_computation.2 | async-start | bytes 10616832 | tf_op jit(solution)/shard_map/all_gather | solution.py:69
  8.0 217.1 %all-gather.8.cloned.1.call-start = ((), (), s32[]{:S(2)}) async-start(), calls=%async_computation.3 | async-start | bytes 2654208 | tf_op jit(solution)/shard_map/all_gather | solution.py:84
  8.7 356.5 %all-reduce.2.cloned.1.call-start = ((), (), s32[]{:S(2)}) async-start(), calls=%async_computation.4 | async-start | bytes 4718592 | tf_op jit(solution)/shard_map/psum | solution.py:90
  9.3 215.8 %copy-start.2 = (f32[1536]{0:T(1024)S(1)}, f32[1536]{0:T(1024)}, u32[]{:S(2)}) copy-start(f32[1536]{0:T(1024)} %param.13) | copy-start | bytes 18436
  227.2 3.5 copy-start.5
  365.3 4.0 copy-start
Sparse Core Ops, SparseCore 0:
  9.0 93.4 all-gather.3
  104.1 89.1 all-gather.5
  195.0 30.0 all-gather.7
  230.8 134.3 all-reduce.1
where the time goes:
time: 424 us; the launch traced here: 415 us
  waiting for transfers between devices  295 us (70%)
  matrix products  53.1 us (13%)
  blocking collectives  48.4 us (11%)
  between operations  14.2 us (3%)
    psum x1, waiting for transfers between devices, on_device(): full_sums, average_sum = lax.psum((products, column_sum), ('dp', 'fsdp'))  94.1 us
    all_gather x1, waiting for transfers between devices, on_device(): lax.all_gather(up_weight, 'fsdp', axis=0, tiled=True)  93.2 us
    all_gather x1, waiting for transfers between devices, on_device(): lax.all_gather(down_weight, 'fsdp', axis=0, tiled=True)  90.9 us
    psum x1, blocking collectives, on_device(): full_sums, average_sum = lax.psum((products, column_sum), ('dp', 'fsdp'))  40.2 us
    dot_general x1, matrix products, on_device(): jnp.dot(columns, lax.all_gather(down_weight, 'fsdp', axis=0, tiled=True),...  16.5 us
    all_gather x1, waiting for transfers between devices, on_device(): lax.all_gather(proj_weight, 'fsdp', axis=0, tiled=True)  14.8 us
    dot_general x2, matrix products, newton_update(): jnp.dot(iterate_rows, covariance, precision=PRECISE, preferred_element_ty...  13.1 us
    dot_general x2, matrix products, newton_update(): jnp.dot(jnp.dot(iterate_rows, covariance, precision=PRECISE, preferred_el...  13 us
  transfers between devices with their start and end apart: 4, of which 4 were waited for; matrix products, arithmetic and copies ran while one was open for 4% of the time, Pallas kernels for 0%

commit v1 on v0

--- a/solution.py
+++ b/solution.py
@@ -1,3 +1,4 @@
+import functools
 import jax
 import jax.numpy as jnp
 from jax import lax
@@ -7,6 +8,33 @@
 RIDGE_TERM = 1.0
 EPSILON = 1e-06
 PRECISE = lax.Precision.HIGHEST
+
+
+def page_drive(v0, dim_i):
+    mid_arr = list(v0.shape[1:])
+    mid_arr[dim_i] *= v0.shape[0]
+    return jnp.moveaxis(v0, 0, dim_i).reshape(mid_arr)
+
+
+def unite_stacks_all_here(row_data, lane_axis):
+    e_next, piece_now = (lax.axis_size(lane_axis), lax.axis_index(lane_axis))
+    w1, state_next = (row_data[None], 1)
+    while state_next < e_next:
+        copies = []
+        for tick in tuple(range(e_next)):
+            copies.append((tick, tick ^ state_next))
+        last = lax.ppermute(w1, lane_axis, copies)
+        z_new = piece_now & state_next == 0
+        w1 = jnp.concatenate([jnp.where(z_new, w1, last), jnp.where(z_new, last, w1)])
+        state_next *= 2
+    return w1
+
+
+def units_read(a0, field_in, dim_k):
+    return page_drive(unite_stacks_all_here(a0, field_in), dim_k)
+
+
+save_panel = functools.partial(units_read, field_in="fsdp", dim_k=0)
 
 
 def rms_scale(values, gain_vector):
@@ -57,11 +85,7 @@
     seq_len = tok_rows // pass_rows
     normed = rms_scale(hidden.astype(jnp.float32), norm_gain).astype(jnp.bfloat16)
     columns = normed
-    hidden_pre = jnp.dot(
-        columns,
-        lax.all_gather(up_weight, "fsdp", axis=0, tiled=True),
-        preferred_element_type=jnp.float32,
-    )
+    hidden_pre = jnp.dot(columns, save_panel(up_weight), preferred_element_type=jnp.float32)
     activated = jax.nn.gelu(hidden_pre, approximate=True).astype(jnp.bfloat16)
     columns = activated
     branch = jnp.dot(

time: 424 us -> 599 us (1.41)
  waiting for transfers between devices: 295 us -> 448 us
  other arithmetic: 3.85 us -> 19.4 us
    ppermute x0 -> x3, waiting for transfers between devices: none -> 351 us  [unite_stacks_all_here(): last = lax.ppermute(w1, lane_axis, copies)]
    all_gather x1 -> x0, waiting for transfers between devices: 93.2 us -> none  [on_device(): lax.all_gather(up_weight, 'fsdp', axis=0, tiled=True)]
    all_gather x1, waiting for transfers between devices: 90.9 us -> 0.01 us  [on_device(): lax.all_gather(down_weight, 'fsdp', axis=0, tiled=True)]
    all_gather x1, waiting for transfers between devices: 14.8 us -> 0.02 us  [on_device(): lax.all_gather(proj_weight, 'fsdp', axis=0, tiled=True)]
    select_n x0 -> x3, other arithmetic: none -> 7.07 us  [unite_stacks_all_here(): jnp.where(z_new, w1, last)]
    concatenate x0 -> x3, other arithmetic: none -> 7.04 us  [unite_stacks_all_here(): jnp.concatenate([jnp.where(z_new, w1, last), jnp.where(z_new, last, w1)])]
  transfers between devices with their start and end apart: 4 -> 6, of which waited for: 4 -> 4; matrix products, arithmetic and copies ran while one was open for 4% -> 6% of each run, Pallas kernels for 0% -> 0%
where the time goes in v1:
time: 599 us; the launch traced here: 589 us
  waiting for transfers between devices  448 us (75%)
  matrix products  53 us (9%)
  blocking collectives  47.3 us (8%)
  other arithmetic  19.4 us (3%)
  between operations  14.5 us (2%)
    ppermute x3, waiting for transfers between devices, unite_stacks_all_here(): last = lax.ppermute(w1, lane_axis, copies)  351 us
    psum x1, waiting for transfers between devices, on_device(): full_sums, average_sum = lax.psum((products, column_sum), ('dp', 'fsdp'))  96.3 us
    psum x1, blocking collectives, on_device(): full_sums, average_sum = lax.psum((products, column_sum), ('dp', 'fsdp'))  39.1 us
    dot_general x1, matrix products, on_device(): jnp.dot(columns, lax.all_gather(down_weight, 'fsdp', axis=0, tiled=True),...  16.5 us
    dot_general x2, matrix products, newton_update(): jnp.dot(iterate_rows, covariance, precision=PRECISE, preferred_element_ty...  13.1 us
    dot_general x2, matrix products, newton_update(): jnp.dot(jnp.dot(iterate_rows, covariance, precision=PRECISE, preferred_el...  12.9 us
  transfers between devices with their start and end apart: 6, of which 4 were waited for; matrix products, arithmetic and copies ran while one was open for 6% of the time, Pallas kernels for 0%

profile of v1, /device:TPU:0, one launch (start us, length us, event | category | flops | bytes accessed | tf_op | source)
XLA Modules:
  0.0 589.1 jit_solution(15190138149387936655)
XLA Ops:
  6.5 0.0 all-gather.3.cloned.1.call-start
  6.5 0.7 all-gather.3.cloned.1.call-update
  7.3 0.0 all-gather.5.cloned.1.call-start
  7.3 0.5 collective-permute-start
  7.8 2.7 collective-permute-done
  10.5 1.4 broadcast_select_fusion.5
  11.9 0.0 copy-start.1
  11.9 0.2 pad_maximum_fusion.2
  12.2 0.8 copy-done.1
  13.0 2.9 collective-permute-start.1
  15.9 127.5 %collective-permute-done.1 = bf16[2,192,3072]{2,1,0:T(8,128)(2,1)} collective-permute-done((bf16[2,192,3072]{2,1,0:T(8,128)(2,1)S(1)}, bf16[2,192,3072]{2,1,0:T(8,128)(2,1)}, u32[]{:S(2)}, u32[]{:S(2)}) %collective-permute-start.1) | collective-permute-done | bytes 2359328 | tf_op jit(solution)/shard_map/ppermute | solution.py:26
  143.4 2.3 broadcast_select_fusion.3
  145.7 0.0 copy-start
  145.7 0.0 copy-start.5
  145.7 2.8 pad_maximum_fusion.1
  148.5 0.0 copy-done
  148.6 1.7 collective-permute-start.2
  150.3 0.0 all-gather.5.cloned.1.call-update
  150.3 0.0 all-reduce.2.cloned.1.call-start
  150.4 0.0 copy-done.5
  150.4 1.8 fusion.8
  152.2 220.9 %collective-permute-done.2 = bf16[4,192,3072]{2,1,0:T(8,128)(2,1)} collective-permute-done((bf16[4,192,3072]{2,1,0:T(8,128)(2,1)}, bf16[4,192,3072]{2,1,0:T(8,128)(2,1)}, u32[]{:S(2)}, u32[]{:S(2)}) %collective-permute-start.2) | collective-permute-done | bytes 4718624 | tf_op jit(solution)/shard_map/ppermute | solution.py:26
  373.2 3.4 broadcast_select_fusion.1
  376.5 0.0 copy-start.3
  376.6 0.0 copy-start.6
  376.6 4.0 pad_maximum_fusion
  380.6 0.0 all-gather.3.cloned.1.call-done
  380.6 0.0 copy-done.3
  380.6 0.0 copy-done.6
  380.6 0.0 copy-start.4
  380.6 16.5 %fusion.16 = bf16[512,1536]{1,0:T(8,128)(2,1)S(1)} fusion(bf16[3072,1536]{1,0:T(8,128)(2,1)} %all-gather.3.cloned.1.call-done, bf16[512,1536]{1,0:T(8,128)(2,1)S(1)} %copy-done.3, bf16[1536,3072]{1,0:T(8,128)(2,1)} %bitcast.24, f32[1536]{0:T(1024)S(1)} %copy-done.6, f32[512]{0:T(512)S(1)} %add_rsqrt_fusion), kind=kOutput, calls=%fused_computation.23 | convolution fusion | flops 9683337216 | bytes 22028288 | tf_op jit(solution)/shard_map/dot_general | solution.py:91
  397.1 0.5 multiply_reduce_fusion.1
  397.6 0.0 all-gather.5.cloned.1.call-done
  397.6 0.0 copy-done.4
  397.6 2.1 fusion.73
  399.8 0.0 copy-start.7
  399.8 3.5 fusion.74
  403.2 0.0 all-reduce.2.cloned.1.call-update
  403.3 0.0 copy-done.7
  403.3 0.2 convert_reduce_fusion
  403.5 39.1 %psum.14 = f32[768]{0:T(1024)S(1)} all-reduce(f32[768]{0:T(1024)S(1)} %get-tuple-element.13), channel_id=1, replica_groups=mesh['dp'=4,'fsdp'=8] {'dp','fsdp'}, use_global_device_ids=true, to_apply=%region_4.5 | all-reduce | flops 768 | bytes 6144 | tf_op jit(solution)/shard_map/psum | solution.py:114
  442.6 96.3 %all-reduce.2.cloned.1.call-done = f32[768,768]{1,0:T(8,128)} async-done(((f32[768,768]{1,0:T(8,128)}), f32[768,768]{1,0:T(8,128)}) %all-reduce.2.cloned.1.call-update) | async-done | bytes 2359312 | tf_op jit(solution)/shard_map/psum | solution.py:114
  538.9 0.0 copy-start.2
  538.9 3.2 multiply_reduce_fusion
  542.8 0.0 copy-done.2
  542.9 6.7 %fusion.19 = f32[768,768]{1,0:T(8,128)S(1)} fusion(f32[]{:T(128)S(6)} %mul.135, f32[]{:T(128)S(6)} %div.58, f32[768,768]{1,0:T(8,128)S(1)} %copy-done.2, f32[768]{0:T(1024)S(1)} %broadcast_multiply_fusion), kind=kOutput, calls=%fused_computation.34 | convolution fusion | flops 5445255168 | bytes 4721672 | tf_op jit(solution)/shard_map/dot_general | solution.py:61
  549.6 6.9 %multiply_subtract_fusion.1 = f32[768,768]{1,0:T(8,128)S(1)} fusion(f32[768,768]{1,0:T(8,128)S(1)} %fusion.19, f32[]{:T(128)S(6)} %mul.135, f32[]{:T(128)S(6)} %div.58, f32[768]{0:T(1024)S(1)} %broadcast_multiply_fusion, f32[768,768]{1,0:T(8,128)S(1)} %copy-done.2), kind=kOutput, calls=%fused_computation.26 | convolution fusion | flops 5448794112 | bytes 7080968 | tf_op jit(solution)/shard_map/dot_general | solution.py:60
  556.5 6.4 %fusion.72 = f32[768,768]{1,0:T(8,128)S(1)} fusion(f32[768,768]{1,0:T(8,128)S(1)} %multiply_subtract_fusion.1, f32[768,768]{1,0:T(8,128)S(1)} %copy-done.2, f32[768]{0:T(1024)S(1)} %broadcast_multiply_fusion), kind=kOutput, calls=%fused_computation.98 | convolution fusion | flops 5439356928 | bytes 7080960 | tf_op jit(solution)/shard_map/dot_general | solution.py:61
  562.8 6.1 %multiply_subtract_fusion = f32[768,768]{1,0:T(8,128)S(1)} fusion(f32[768,768]{1,0:T(8,128)S(1)} %multiply_subtract_fusion.1, f32[768,768]{1,0:T(8,128)S(1)} %fusion.72), kind=kOutput, calls=%fused_computation.25 | convolution fusion | flops 5436997632 | bytes 7077888 | tf_op jit(solution)/shard_map/dot_general | solution.py:60
  568.9 1.5 fusion.41
  570.4 1.6 fusion.71
  572.0 1.3 fusion.39
  573.2 0.1 fusion.38
  573.4 8.1 %all_to_all.12 = bf16[4,8,768]{2,1,0:T(8,128)(2,1)S(1)} all-to-all(bf16[4,8,768]{2,1,0:T(8,128)(2,1)S(1)} %fusion.38), channel_id=1, replica_groups=mesh['dp'=4,'fsdp'=8] {'dp'}, dimensions={0} | all-to-all | bytes 98304 | tf_op jit(solution)/shard_map/all_to_all | solution.py:129
  581.5 0.6 copy.11
  (8 shorter events, 0.0 us)
Async XLA Ops:
  6.5 374.1 %all-gather.3.cloned.1.call-start = ((), (), s32[]{:S(2)}) async-start(), calls=%async_computation.1 | async-start | bytes 10616832 | tf_op jit(solution)/shard_map/all_gather | solution.py:93
  7.3 390.3 %all-gather.5.cloned.1.call-start = ((), (), s32[]{:S(2)}) async-start(), calls=%async_computation.2 | async-start | bytes 2654208 | tf_op jit(solution)/shard_map/all_gather | solution.py:108
  7.3 3.2 collective-permute-start
  11.9 1.0 copy-start.1
  13.0 130.4 %collective-permute-start.1 = (bf16[2,192,3072]{2,1,0:T(8,128)(2,1)S(1)}, bf16[2,192,3072]{2,1,0:T(8,128)(2,1)}, u32[]{:S(2)}, u32[]{:S(2)}) collective-permute-start(bf16[2,192,3072]{2,1,0:T(8,128)(2,1)S(1)} %pad_maximum_fusion.2), channel_id=1, source_target_pairs={{0,2},{1,3},{2,0},{3,1},{4,6},{5,7},{6,4},{7,5},{8,10},{9,11},{10,... | collective-permute-start | bytes 7077896 | tf_op jit(solution)/shard_map/ppermute | solution.py:26
  145.7 2.8 copy-start
  145.7 4.7 copy-start.5
  148.6 224.6 %collective-permute-start.2 = (bf16[4,192,3072]{2,1,0:T(8,128)(2,1)}, bf16[4,192,3072]{2,1,0:T(8,128)(2,1)}, u32[]{:S(2)}, u32[]{:S(2)}) collective-permute-start(bf16[4,192,3072]{2,1,0:T(8,128)(2,1)} %pad_maximum_fusion.1), channel_id=1, source_target_pairs={{0,4},{1,5},{2,6},{3,7},{4,0},{5,1},{6,2},{7,3},{8,12},{9,13},{10,... | collective-permute-start | bytes 14155784 | tf_op jit(solution)/shard_map/ppermute | solution.py:26
  150.3 388.5 %all-reduce.2.cloned.1.call-start = ((), (), s32[]{:S(2)}) async-start(), calls=%async_computation.3 | async-start | bytes 4718592 | tf_op jit(solution)/shard_map/psum | solution.py:114
  376.5 4.1 copy-start.3
  376.6 4.1 copy-start.6
  380.6 17.0 %copy-start.4 = (f32[1536]{0:T(1024)S(1)}, f32[1536]{0:T(1024)}, u32[]{:S(2)}) copy-start(f32[1536]{0:T(1024)} %param.13) | copy-start | bytes 18436
  399.8 3.5 copy-start.7
  538.9 4.0 copy-start.2
Sparse Core Ops, SparseCore 0:
  9.0 133.6 all-gather.2
  150.4 133.4 all-gather.4
  403.4 135.4 all-reduce.1
